TPU v7x, 32 devices: a whole 2x2x4 slice. The times are simulated.
32 devices in a mesh: fsdp: 8 (over z, x), seq: 4 (over y, core).
Axes of the slice: x: 2, y: 2, z: 4, core: 2. Of those that a mesh axis runs over, the one named last changes fastest.
Arguments:
- residual: bfloat16 [24, 1024, 767], P('fsdp', 'seq'), may hold values from -6 to 6
- out_grad: bfloat16 [24, 1024, 767], P('fsdp', 'seq'), may hold values from -6 to 6
- doc_lengths: int32 [24, 8], P('fsdp'), may hold values from 1 to 512, 1024 in all within a row
- gain_one: float32 [768], replicated, may hold values from 0.5 to 1.5
- qkv_weight: float32 [768, 2304], P('fsdp'), may hold values from -0.21875 to 0.21875
- qv_bias: float32 [12, 128], replicated, may hold values from -3 to 3
- out_weight: float32 [768, 767], P('fsdp'), may hold values from -0.875 to 0.875
- out_bias: float32 [767], replicated, may hold values from -3 to 3
- gain_two: float32 [768], replicated, may hold values from 0.5 to 1.5
- fc_weight: float32 [768, 3072], P('fsdp'), may hold values from -0.21875 to 0.21875
- fc_bias: float32 [3072], replicated, may hold values from -3 to 3
- proj_weight: float32 [3072, 767], P('fsdp'), may hold values from -0.15625 to 0.15625
- proj_bias: float32 [767], replicated, may hold values from -3 to 3
Outputs:
- output: bfloat16 [24, 1024, 767], P('fsdp', 'seq')
- input_grad: float32 [24, 1024, 767], P('fsdp', 'seq')
- gain_one_grad: float32 [768], replicated
- qkv_weight_grad: float32 [768, 2304], P('fsdp')
- qv_bias_grad: float32 [12, 128], replicated
- out_weight_grad: float32 [768, 767], P('fsdp')
- out_bias_grad: float32 [767], replicated
- gain_two_grad: float32 [768], replicated
- fc_weight_grad: float32 [768, 3072], P('fsdp')
- fc_bias_grad: float32 [3072], replicated
- proj_weight_grad: float32 [3072, 767], P('fsdp')
- proj_bias_grad: float32 [767], replicated
Inputs may be any that keep to these rules, and one draw needn't show every extreme that they name: `doc_lengths`: each sequence's 8 document lengths sum to 1024; the longest is exactly 512 tokens.
All inputs are finite; a program needn't handle non-finite values.
Results may differ from a plain program's by a relative error of at most 0.014.
Values may be sent and summed in bfloat16 or wider, within the bound.
No kernel may reach another device: no remote copies, remote signals or barrier semaphores. Data moves between devices by JAX's collectives and lax.ppermute only.
A program may use at most 320 MiB of HBM per device.

v0:
```python
import functools
import jax
import jax.numpy as jnp
from jax import lax
from jax.sharding import PartitionSpec as P

EPS = 1e-06


def centred_norm(residual, gain):
    row_total = jnp.sum(residual, axis=-1, keepdims=True)
    full_row = jnp.concatenate([residual, -row_total], axis=-1)
    inv_rms = lax.rsqrt(jnp.mean(full_row * full_row, axis=-1, keepdims=True) + EPS)
    return full_row * inv_rms * gain


def document_index(lengths, length):
    starts = jnp.cumsum(lengths, axis=1) - lengths
    position = jnp.arange(length, dtype=jnp.int32)
    inside = (position[None, :, None] >= starts[:, None, :]).astype(jnp.int32)
    return jnp.sum(inside, axis=2) - 1


def masked_scores(queries, key_rows, doc_ids, first_row, row_count, factor):
    scores = factor * jnp.einsum(
        "bqhe,bkhe->bhqk", queries, key_rows, preferred_element_type=jnp.float32
    )
    length = key_rows.shape[1]
    row_pos = first_row + jnp.arange(row_count, dtype=jnp.int32)
    col_pos = jnp.arange(length, dtype=jnp.int32)
    row_ids = doc_ids[:, first_row : first_row + row_count]
    allowed = (row_ids[:, :, None] == doc_ids[:, None, :]) & (
        col_pos[None, None, :] <= row_pos[None, :, None]
    )
    return jnp.where(allowed[:, None], scores, -1e30)


def local(
    residual,
    out_grad,
    doc_lengths,
    gain_one,
    qkv_weight,
    qv_bias,
    out_weight,
    out_bias,
    gain_two,
    fc_weight,
    fc_bias,
    proj_weight,
    proj_bias,
):
    ranks = lax.axis_size("seq")
    seq_count, local_len, narrow = residual.shape
    width = narrow + 1
    full_len = local_len * ranks
    heads_all = qv_bias.shape[0]
    head_dim = qv_bias.shape[1] // 2
    my_heads = heads_all // ranks
    token_count = seq_count * local_len
    factor = head_dim ** (-0.5)
    block_rows = min(512, full_len)
    qkv_matrix, out_matrix, fc_matrix, proj_matrix = (
        lax.all_gather(qkv_weight.astype(jnp.bfloat16), "fsdp", axis=0, tiled=True),
        lax.all_gather(out_weight.astype(jnp.bfloat16), "fsdp", axis=0, tiled=True),
        lax.all_gather(fc_weight.astype(jnp.bfloat16), "fsdp", axis=0, tiled=True),
        lax.all_gather(proj_weight.astype(jnp.bfloat16), "fsdp", axis=0, tiled=True),
    )
    resid_flat = residual.astype(jnp.float32).reshape(token_count, narrow)
    normed_one = centred_norm(resid_flat, gain_one).astype(jnp.bfloat16)
    zero_part = jnp.zeros((heads_all, head_dim), jnp.float32)
    bias_full = jnp.stack(
        [qv_bias[:, :head_dim], zero_part, qv_bias[:, head_dim:]], axis=1
    ).reshape(3 * width)
    packed = (
        jnp.dot(normed_one, qkv_matrix, preferred_element_type=jnp.float32) + bias_full
    ).astype(jnp.bfloat16)
    packed = packed.reshape(seq_count, local_len, ranks, my_heads * 3 * head_dim)
    by_heads = lax.all_to_all(packed, "seq", split_axis=2, concat_axis=1, tiled=True)
    by_heads = by_heads.reshape(seq_count, full_len, my_heads, 3, head_dim)
    queries = by_heads[:, :, :, 0]
    key_rows = by_heads[:, :, :, 1]
    value_rows = by_heads[:, :, :, 2]
    doc_ids = document_index(doc_lengths, full_len)
    outputs_list = []
    lse_list = []
    for first_row in range(0, full_len, block_rows):
        scores = masked_scores(
            queries[:, first_row : first_row + block_rows],
            key_rows,
            doc_ids,
            first_row,
            block_rows,
            factor,
        )
        row_max = jnp.max(scores, axis=-1, keepdims=True)
        exp_scores = jnp.exp(scores - row_max)
        row_total = jnp.sum(exp_scores, axis=-1, keepdims=True)
        prob_low = (exp_scores / row_total).astype(jnp.bfloat16)
        lse_list.append(row_max + jnp.log(row_total))
        outputs_list.append(
            jnp.einsum("bhqk,bkhe->bqhe", prob_low, value_rows, preferred_element_type=jnp.float32)
        )
    attended = jnp.concatenate(outputs_list, axis=1).astype(jnp.bfloat16)
    attended = attended.reshape(seq_count, full_len, my_heads * head_dim)
    by_tokens = lax.all_to_all(attended, "seq", split_axis=1, concat_axis=2, tiled=True)
    attn_flat = by_tokens.reshape(token_count, width)
    middle = (
        resid_flat + jnp.dot(attn_flat, out_matrix, preferred_element_type=jnp.float32) + out_bias
    )
    normed_two = centred_norm(middle, gain_two).astype(jnp.bfloat16)
    pre_act = jnp.dot(normed_two, fc_matrix, preferred_element_type=jnp.float32) + fc_bias
    hidden = jax.nn.gelu(pre_act, approximate=True).astype(jnp.bfloat16)
    output = middle + jnp.dot(hidden, proj_matrix, preferred_element_type=jnp.float32) + proj_bias
    output = output.astype(jnp.bfloat16).reshape(seq_count, local_len, narrow)
    qkv_matrix, out_matrix, fc_matrix, proj_matrix = (
        lax.all_gather(qkv_weight.astype(jnp.bfloat16), "fsdp", axis=0, tiled=True),
        lax.all_gather(out_weight.astype(jnp.bfloat16), "fsdp", axis=0, tiled=True),
        lax.all_gather(fc_weight.astype(jnp.bfloat16), "fsdp", axis=0, tiled=True),
        lax.all_gather(proj_weight.astype(jnp.bfloat16), "fsdp", axis=0, tiled=True),
    )
    grad_low = out_grad.reshape(token_count, narrow)
    grad_flat = grad_low.astype(jnp.float32)
    proj_grad = jnp.einsum("tf,tc->fc", hidden, grad_low, preferred_element_type=jnp.float32)
    proj_bias_grad = jnp.sum(grad_flat, axis=0)
    d_hidden = jnp.einsum("tc,fc->tf", grad_low, proj_matrix, preferred_element_type=jnp.float32)
    gelu_value, gelu_back = jax.vjp(functools.partial(jax.nn.gelu, approximate=True), pre_act)
    d_pre = gelu_back(d_hidden)[0].astype(jnp.bfloat16)
    fc_grad = jnp.einsum("td,tf->df", normed_two, d_pre, preferred_element_type=jnp.float32)
    fc_bias_grad = jnp.sum(d_pre.astype(jnp.float32), axis=0)
    d_norm_two = jnp.einsum("tf,df->td", d_pre, fc_matrix, preferred_element_type=jnp.float32)
    second_value, second_back = jax.vjp(centred_norm, middle, gain_two)
    d_mid_part, gain_two_grad = second_back(d_norm_two)
    d_middle = grad_flat + d_mid_part
    d_branch = d_middle.astype(jnp.bfloat16)
    out_weight_part = jnp.einsum(
        "td,tc->dc", attn_flat, d_branch, preferred_element_type=jnp.float32
    )
    out_bias_grad = jnp.sum(d_branch.astype(jnp.float32), axis=0)
    d_attn = jnp.einsum(
        "tc,dc->td", d_branch, out_matrix, preferred_element_type=jnp.float32
    ).astype(jnp.bfloat16)
    d_attn = d_attn.reshape(seq_count, local_len, ranks, my_heads * head_dim)
    d_heads = lax.all_to_all(d_attn, "seq", split_axis=2, concat_axis=1, tiled=True)
    d_heads = d_heads.reshape(seq_count, full_len, my_heads, head_dim)
    key_grad = jnp.zeros((seq_count, full_len, my_heads, head_dim), jnp.float32)
    value_grad = jnp.zeros((seq_count, full_len, my_heads, head_dim), jnp.float32)
    query_parts = []
    for block_index, first_row in enumerate(range(0, full_len, block_rows)):
        query_block = queries[:, first_row : first_row + block_rows]
        grad_block = d_heads[:, first_row : first_row + block_rows]
        scores = masked_scores(query_block, key_rows, doc_ids, first_row, block_rows, factor)
        prob_full = jnp.exp(scores - lse_list[block_index])
        prob_low = prob_full.astype(jnp.bfloat16)
        d_probs = jnp.einsum(
            "bqhe,bkhe->bhqk", grad_block, value_rows, preferred_element_type=jnp.float32
        )
        row_delta = jnp.sum(prob_full * d_probs, axis=-1, keepdims=True)
        d_scores = (prob_full * (d_probs - row_delta)).astype(jnp.bfloat16)
        query_parts.append(
            factor
            * jnp.einsum("bhqk,bkhe->bqhe", d_scores, key_rows, preferred_element_type=jnp.float32)
        )
        key_grad = key_grad + factor * jnp.einsum(
            "bhqk,bqhe->bkhe", d_scores, query_block, preferred_element_type=jnp.float32
        )
        value_grad = value_grad + jnp.einsum(
            "bhqk,bqhe->bkhe", prob_low, grad_block, preferred_element_type=jnp.float32
        )
    query_grad = jnp.concatenate(query_parts, axis=1)
    d_packed = jnp.stack([query_grad, key_grad, value_grad], axis=3).astype(jnp.bfloat16)
    d_packed = d_packed.reshape(seq_count, full_len, my_heads * 3 * head_dim)
    d_tokens = lax.all_to_all(d_packed, "seq", split_axis=1, concat_axis=2, tiled=True)
    d_tokens = d_tokens.reshape(token_count, 3 * width)
    qkv_grad = jnp.einsum("td,tc->dc", normed_one, d_tokens, preferred_element_type=jnp.float32)
    column_sums = jnp.sum(d_tokens.astype(jnp.float32), axis=0).reshape(heads_all, 3, head_dim)
    qv_bias_grad = jnp.concatenate([column_sums[:, 0], column_sums[:, 2]], axis=1)
    d_norm_one = jnp.einsum("tc,dc->td", d_tokens, qkv_matrix, preferred_element_type=jnp.float32)
    first_value, first_back = jax.vjp(centred_norm, resid_flat, gain_one)
    d_resid_part, gain_one_grad = first_back(d_norm_one)
    input_grad = (d_middle + d_resid_part).reshape(seq_count, local_len, narrow)
    qkv_share, out_share, fc_share, proj_share = (
        lax.psum_scatter(qkv_grad, "fsdp", scatter_dimension=0, tiled=True),
        lax.psum_scatter(out_weight_part, "fsdp", scatter_dimension=0, tiled=True),
        lax.psum_scatter(fc_grad, "fsdp", scatter_dimension=0, tiled=True),
        lax.psum_scatter(proj_grad, "fsdp", scatter_dimension=0, tiled=True),
    )
    qkv_share, out_share, fc_share, proj_share = (
        lax.psum(qkv_share.astype(jnp.bfloat16), "seq").astype(jnp.float32),
        lax.psum(out_share.astype(jnp.bfloat16), "seq").astype(jnp.float32),
        lax.psum(fc_share.astype(jnp.bfloat16), "seq").astype(jnp.float32),
        lax.psum(proj_share.astype(jnp.bfloat16), "seq").astype(jnp.float32),
    )
    vector_sums = lax.psum(
        (gain_one_grad, qv_bias_grad, out_bias_grad, gain_two_grad, fc_bias_grad, proj_bias_grad),
        ("fsdp", "seq"),
    )
    return (
        output,
        input_grad,
        vector_sums[0],
        qkv_share,
        vector_sums[1],
        out_share,
        vector_sums[2],
        vector_sums[3],
        fc_share,
        vector_sums[4],
        proj_share,
        vector_sums[5],
    )


def solution(mesh):
    return jax.shard_map(
        local,
        mesh=mesh,
        in_specs=(
            P("fsdp", "seq", None),
            P("fsdp", "seq", None),
            P("fsdp", None),
            P(),
            P("fsdp", None),
            P(),
            P("fsdp", None),
            P(),
            P(),
            P("fsdp", None),
            P(),
            P("fsdp", None),
            P(),
        ),
        out_specs=(
            P("fsdp", "seq", None),
            P("fsdp", "seq", None),
            P(),
            P("fsdp", None),
            P(),
            P("fsdp", None),
            P(),
            P(),
            P("fsdp", None),
            P(),
            P("fsdp", None),
            P(),
        ),
        check_vma=False,
    )
```

profile of v0, /device:TPU:0, one launch (start us, length us, event | category | flops | bytes accessed | tf_op | source)
XLA Modules:
  0.0 1041.5 jit_solution(17890892516380688609)
XLA Ops:
  7.2 2.1 convert_element_type.113
  15.6 63.1 %all-gather.5.cloned.1.call-done = bf16[768,2304]{1,0:T(8,128)(2,1)} async-done(((bf16[96,2304]{1,0:T(8,128)(2,1)}), bf16[768,2304]{1,0:T(8,128)(2,1)}) %all-gather.5.cloned.1.call-update) | async-done | bytes 3538960 | tf_op jit(solution)/shard_map/all_gather | solution.py:64
  78.7 6.6 add_convert_fusion
  85.3 9.1 reshape.215
  94.4 7.9 copy.69
  102.3 3.8 all-to-all-start
  106.2 2.1 convert_element_type.122
  109.2 3.8 compare_and_fusion.1
  113.0 34.3 %all-to-all-done = bf16[3,256,4,576]{1,3,0,2:T(8,128)(2,1)S(1)} async-done(((bf16[3,256,4,576]{1,3,0,2:T(8,128)(2,1)}), bf16[3,256,4,576]{1,3,0,2:T(8,128)(2,1)S(1)}, u32[]{:S(2)}, u32[]{:S(2)}) %all-to-all-start) | async-done | bytes 3538976 | tf_op jit(solution)/shard_map/all_to_all | solution.py:79
  147.2 4.5 copy.70
  151.8 6.1 reshape.216
  159.8 9.2 fusion.57
  169.0 10.1 fusion.1
  179.0 9.0 fusion.28
  188.1 2.7 copy.75
  190.7 10.6 %fusion.58 = (f32[3,3,512]{2,1,0:T(4,128)}, f32[3,3,512,1024]{3,2,1,0:T(8,128)}) fusion(bf16[3,1024,3,3,64]{1,4,3,2,0:T(8,128)(2,1)S(1)} %reshape.216, bf16[3,1024,3,64]{1,3,2,0:T(8,128)(2,1)} %copy-done.13, pred[3,512,1024]{2,1,0:T(8,128)(4,1)} %get-tuple-element.34), kind=kOutput, calls=%fused_computation.122 | convolution fusion | flops 618130944 | bytes 22235136 | tf_op jit(solution)/shard_map/bqhe,bkhe->bhqk/dot_general | solution.py:25
  201.3 10.0 fusion
  211.3 9.0 fusion.29
  220.3 2.3 copy.74
  222.6 3.1 pad_maximum_fusion.3
  225.7 28.3 %all_to_all.60 = bf16[3,1024,192]{2,0,1:T(4,128)(2,1)S(1)} all-to-all(bf16[3,1024,192]{2,0,1:T(4,128)(2,1)S(1)} %pad_maximum_fusion.3), channel_id=1, replica_groups=mesh['fsdp'=8,'seq'=4] {'seq'}, dimensions={1} | all-to-all | bytes 2359296 | tf_op jit(solution)/shard_map/all_to_all | solution.py:106
  254.0 2.6 copy.77
  256.6 4.0 reshape.217
  260.6 3.2 fusion.59
  265.6 10.9 %fusion.51 = f32[768,3072]{1,0:T(8,128)} fusion(bf16[768,3072]{1,0:T(8,128)(2,1)} %all-gather.9.cloned.1.call-done, f32[768]{0:T(1024)S(1)} %copy-done.25, f32[768]{0:T(1024)S(1)} %fusion.48, f32[768,1]{1,0:T(8,128)} %copy-done.11, f32[768,767]{1,0:T(8,128)} %copy-done.4), kind=kOutput, calls=%fused_computation.117 | convolution fusion | flops 3626237952 | bytes 16521216 | tf_op jit(solution)/shard_map/dot_general | solution.py:112
  276.5 5.5 all-gather.11.cloned.1.call-done
  282.0 13.7 %convert_reduce_fusion = (f32[3072]{0:T(1024)}, bf16[768,3072]{1,0:T(8,128)(2,1)S(1)}) fusion(f32[768,3072]{1,0:T(8,128)} %fusion.51, f32[3072]{0:T(1024)} %param.23, bf16[768,767]{1,0:T(8,128)(2,1)} %bitcast.116, bf16[3072,767]{1,0:T(8,128)(2,1)} %all-gather.11.cloned.1.call-done), kind=kOutput, calls=%fused_computation.27 | convolution fusion | flops 3673420800 | bytes 20070912 | tf_op jit(solution)/shard_map/tc,fc->tf/dot_general | solution.py:126
  295.7 4.8 multiply_reduce_fusion.2
  303.9 2.1 convolution_convert_fusion
  306.0 4.4 reshape.220
  310.4 3.5 copy.79
  314.0 4.3 all-to-all-start.2
  321.1 4.1 fusion.60
  325.3 8.9 all-to-all-done.2
  334.2 3.2 copy.80
  337.4 3.8 reshape.221
  341.2 8.6 fusion.11
  349.9 15.6 %multiply_reduce_fusion = (f32[3,3,512]{2,1,0:T(4,128)S(1)}, f32[3,3,512,1024]{3,2,1,0:T(8,128)}) fusion(f32[3,3,512,1024]{3,2,1,0:T(8,128)} %get-tuple-element.41, f32[3,3,512]{2,1,0:T(4,128)S(1)} %copy-done.21, bf16[3,1024,3,3,64]{1,4,3,2,0:T(8,128)(2,1)S(1)} %reshape.216, bf16[3,1024,3,64]{1,3,2,0:T(8,128)(2,1)S(1)} %copy-done.8), kind=kOutput, calls=%fused_computation.1 | convolution fusion | flops 618130944 | bytes 39561216 | tf_op jit(solution)/shard_map/bqhe,bkhe->bhqk/dot_general | solution.py:155
  365.5 15.5 %multiply_reduce_fusion.1 = (f32[3,3,512]{2,1,0:T(4,128)S(1)}, f32[3,3,512,1024]{3,2,1,0:T(8,128)}) fusion(f32[3,3,512,1024]{3,2,1,0:T(8,128)} %get-tuple-element.43, f32[3,3,512]{2,1,0:T(4,128)S(1)} %copy-done.22, bf16[3,1024,3,3,64]{1,4,3,2,0:T(8,128)(2,1)S(1)} %reshape.216, bf16[3,1024,3,64]{1,3,2,0:T(8,128)(2,1)S(1)} %copy-done.8), kind=kOutput, calls=%fused_computation.4 | convolution fusion | flops 618130944 | bytes 39561216 | tf_op jit(solution)/shard_map/bqhe,bkhe->bhqk/dot_general | solution.py:155
  381.0 13.1 %multiply_convert_fusion.1 = bf16[3,3,512,1024]{3,2,1,0:T(8,128)(2,1)S(1)} fusion(f32[3,3,512,1024]{3,2,1,0:T(8,128)} %get-tuple-element.48, f32[3,3,512,1024]{3,2,1,0:T(8,128)} %get-tuple-element.43, f32[3,3,512]{2,1,0:T(4,128)S(1)} %get-tuple-element.47, f32[3,3,512]{2,1,0:T(4,128)S(1)} %copy-done.22), kind=kLoop, calls=%fused_computation.3 | loop fusion | flops 18874368 | bytes 47222784 | tf_op jit(solution)/shard_map/convert_element_type | solution.py:159
  394.1 3.1 fusion.33
  399.0 8.3 fusion.24
  407.2 13.1 %multiply_convert_fusion = bf16[3,3,512,1024]{3,2,1,0:T(8,128)(2,1)S(1)} fusion(f32[3,3,512,1024]{3,2,1,0:T(8,128)} %get-tuple-element.50, f32[3,3,512,1024]{3,2,1,0:T(8,128)} %get-tuple-element.41, f32[3,3,512]{2,1,0:T(4,128)S(1)} %get-tuple-element.49, f32[3,3,512]{2,1,0:T(4,128)S(1)} %copy-done.21), kind=kLoop, calls=%fused_computation | loop fusion | flops 18874368 | bytes 47222784 | tf_op jit(solution)/shard_map/convert_element_type | solution.py:159
  420.3 3.0 fusion.32
  426.2 6.2 copy.82
  432.4 63.3 %all_to_all.61 = bf16[3,1024,576]{2,0,1:T(4,128)(2,1)S(1)} all-to-all(bf16[3,1024,576]{2,0,1:T(4,128)(2,1)} %copy.82), channel_id=1, replica_groups=mesh['fsdp'=8,'seq'=4] {'seq'}, dimensions={1} | all-to-all | bytes 7077888 | tf_op jit(solution)/shard_map/all_to_all | solution.py:173
  495.7 6.6 convert_reduce_fusion.1
  502.3 8.0 reshape.222
  510.3 7.6 fusion.49
  519.2 13.5 %fusion.52 = f32[3072,767]{1,0:T(8,128)} fusion(bf16[768,767]{1,0:T(8,128)(2,1)S(1)} %bitcast.117, f32[768,3072]{1,0:T(8,128)} %fusion.51, f32[3072]{0:T(1024)} %param.23), kind=kOutput, calls=%fused_computation.118 | convolution fusion | flops 3642753024 | bytes 20052480 | tf_op jit(solution)/shard_map/tf,tc->fc/dot_general | solution.py:124
  532.8 10.8 %fusion.50 = f32[768,3072]{1,0:T(8,128)} fusion(bf16[768,3072]{1,0:T(8,128)(2,1)} %copy-done.15, f32[768]{0:T(1024)S(1)} %copy-done.25, f32[768]{0:T(1024)S(1)} %fusion.48, f32[768,1]{1,0:T(8,128)} %copy-done.11, f32[768,767]{1,0:T(8,128)} %copy-done.4), kind=kOutput, calls=%fused_computation.116 | convolution fusion | flops 3626237952 | bytes 16521216 | tf_op jit(solution)/shard_map/td,tf->df/dot_general | solution.py:129
  544.8 12.8 %add_convert_fusion.2 = bf16[768,767]{1,0:T(8,128)(2,1)} fusion(f32[768,767]{1,0:T(8,128)} %copy-done.4, bf16[3072,767]{1,0:T(8,128)(2,1)} %all-gather.11.cloned.1.call-done, f32[767]{0:T(1024)S(1)} %copy-done.38, f32[768,3072]{1,0:T(8,128)} %fusion.51, f32[3072]{0:T(1024)} %param.23), kind=kOutput, calls=%fused_computation.55 | convolution fusion | flops 3644520192 | bytes 17699324 | tf_op jit(solution)/shard_map/dot_general | solution.py:114
  560.5 8.2 multiply_reduce_fusion.3
  568.7 39.5 %all-reduce = (f32[768]{0:T(1024)}, f32[12,128]{1,0:T(8,128)}, f32[767]{0:T(1024)}, f32[768]{0:T(1024)}, f32[3072]{0:T(1024)}, /*index=5*/f32[767]{0:T(1024)}) all-reduce(f32[768]{0:T(1024)} %get-tuple-element.14, f32[12,128]{1,0:T(8,128)} %pad_maximum_fusion.5, ...), channel_id=1, replica_groups=mesh['fsdp'=8,'seq'=4] {'fsdp','seq'}, use_global_device_ids=true, to_apply=%region_15.16 | all-reduce | flops 7678 | bytes 61424 | tf_op jit(solution)/shard_map/psum | solution.py:194
  610.6 34.1 %reduce-scatter.5.cloned.1.call-done = f32[96,2304]{1,0:T(8,128)} async-done(((f32[768,2304]{1,0:T(8,128)}), f32[96,2304]{1,0:T(8,128)}) %reduce-scatter.5.cloned.1.call-update) | async-done | bytes 884752 | tf_op jit(solution)/shard_map/reduce_scatter | solution.py:183
  644.7 2.0 convert_element_type.133
  646.6 164.6 %reduce-scatter.11.cloned.1.call-done = f32[384,767]{1,0:T(8,128)} async-done(((f32[3072,767]{1,0:T(8,128)}), f32[384,767]{1,0:T(8,128)}) %reduce-scatter.11.cloned.1.call-update) | async-done | bytes 1178128 | tf_op jit(solution)/shard_map/reduce_scatter | solution.py:186
  811.2 2.1 convert_element_type.142
  813.4 164.5 %reduce-scatter.9.cloned.1.call-done = f32[96,3072]{1,0:T(8,128)} async-done(((f32[768,3072]{1,0:T(8,128)}), f32[96,3072]{1,0:T(8,128)}) %reduce-scatter.9.cloned.1.call-update) | async-done | bytes 1179664 | tf_op jit(solution)/shard_map/reduce_scatter | solution.py:185
  977.9 2.2 convert_element_type.139
  980.1 2.4 add_add_fusion
  984.6 42.9 %all-reduce.4.cloned.1.call-done = (bf16[96,2304]{1,0:T(8,128)(2,1)}, bf16[96,767]{1,0:T(8,128)(2,1)}, bf16[96,3072]{1,0:T(8,128)(2,1)}, bf16[384,767]{1,0:T(8,128)(2,1)}) async-done(((bf16[96,2304]{1,0:T(8,128)(2,1)}, bf16[96,767]{1,0:T(8,128)(2,1)}, bf16[96,3072]{1,0:T(8,128)(2,1)}, bf16[384,767]{1,0:T(8,128)(2,1)}), (bf16[96,2304]{1,0:T(8,128)(2,1)}, bf16[96,767]{1,0:T(8,128)(2,1)}, ...) | async-done | bytes 1768528 | tf_op jit(solution)/shard_map/psum | solution.py:189
  1029.3 2.0 convert_element_type.134
  1031.3 2.2 convert_element_type.140
  (148 shorter events, 34.3 us)
Async XLA Ops:
  7.2 4.0 copy-start.18
  7.2 4.9 copy-start.16
  7.2 71.5 %all-gather.5.cloned.1.call-start = ((), (), s32[]{:S(2)}) async-start(), calls=%async_computation.8 | async-start | bytes 3981312 | tf_op jit(solution)/shard_map/all_gather | solution.py:64
  9.4 3.1 copy-start.32
  9.4 251.2 %all-gather.7.cloned.1.call-start = ((), (), s32[]{:S(2)}) async-start(), calls=%async_computation.9 | async-start | bytes 1327104 | tf_op jit(solution)/shard_map/all_gather | solution.py:65
  11.1 254.5 %all-gather.9.cloned.1.call-start = ((), (), s32[]{:S(2)}) async-start(), calls=%async_computation.10 | async-start | bytes 5308416 | tf_op jit(solution)/shard_map/all_gather | solution.py:66
  12.9 65.9 %copy-start.9 = (f32[1,768]{0,1:T(8,128)}, f32[1,768]{0,1:T(8,128)S(1)}, u32[]{:S(2)}) copy-start(f32[1,768]{0,1:T(8,128)S(1)} %copy.93) | copy-start | bytes 9220
  12.9 65.8 %copy-start.26 = (f32[768]{0:T(1024)S(1)}, f32[768]{0:T(1024)}, u32[]{:S(2)}) copy-start(f32[768]{0:T(1024)} %param.16) | copy-start | bytes 9220
  14.5 70.8 %copy-start = (f32[768,767]{1,0:T(8,128)}, f32[768,767]{1,0:T(8,128)S(1)}, u32[]{:S(2)}) copy-start(f32[768,767]{1,0:T(8,128)S(1)} %convert.50) | copy-start | bytes 7068676
  14.8 0.8 copy-start.30
  15.6 69.7 %copy-start.23 = (f32[768]{0:T(1024)}, f32[768]{0:T(1024)S(1)}, u32[]{:S(2)}) copy-start(f32[768]{0:T(1024)S(1)} %fusion.47) | copy-start | bytes 9220
  102.3 45.0 %all-to-all-start = ((bf16[3,256,4,576]{1,3,0,2:T(8,128)(2,1)}), bf16[3,256,4,576]{1,3,0,2:T(8,128)(2,1)S(1)}, u32[]{:S(2)}, u32[]{:S(2)}) async-start(bf16[3,256,4,576]{1,3,0,2:T(8,128)(2,1)} %copy.69), calls=%async_computation | async-start | bytes 7077888 | tf_op jit(solution)/shard_map/all_to_all | solution.py:79
  106.1 2.2 copy-start.34
  106.1 175.9 %all-gather.11.cloned.1.call-start = ((), (), s32[]{:S(2)}) async-start(), calls=%async_computation.11 | async-start | bytes 5308416 | tf_op jit(solution)/shard_map/all_gather | solution.py:67
  157.8 1.9 copy-start.17
  158.0 11.0 %copy-start.13 = (bf16[3,1024,3,64]{1,3,2,0:T(8,128)(2,1)}, bf16[3,1024,3,64]{1,3,2,0:T(8,128)(2,1)S(1)}, u32[]{:S(2)}) copy-start(bf16[3,1024,3,64]{1,3,2,0:T(8,128)(2,1)S(1)} %slice_bitcast_fusion.1) | copy-start | bytes 3538948
  254.0 6.6 copy-start.37
  263.8 1.4 copy-start.4
  263.8 1.8 copy-start.25
  264.0 1.5 copy-start.11
  282.0 13.7 %copy-start.5 = (f32[768,767]{1,0:T(8,128)S(1)}, f32[768,767]{1,0:T(8,128)}, u32[]{:S(2)}) copy-start(f32[768,767]{1,0:T(8,128)} %copy-done.4) | copy-start | bytes 7068676
  282.0 13.7 %copy-start.12 = (f32[768,1]{1,0:T(8,128)S(1)}, f32[768,1]{1,0:T(8,128)}, u32[]{:S(2)}) copy-start(f32[768,1]{1,0:T(8,128)} %copy-done.11) | copy-start | bytes 9220
  282.0 13.7 %copy-start.35 = (bf16[768,3072]{1,0:T(8,128)(2,1)S(1)}, bf16[768,3072]{1,0:T(8,128)(2,1)}, u32[]{:S(2)}) copy-start(bf16[768,3072]{1,0:T(8,128)(2,1)} %all-gather.9.cloned.1.call-done) | copy-start | bytes 14155780
  295.7 4.8 copy-start.15
  300.5 1.3 copy-start.6
  301.1 1.7 copy-start.2
  301.8 1.1 copy-start.28
  301.8 2.1 copy-start.36
  302.9 1.0 copy-start.19
  314.0 20.2 %all-to-all-start.2 = ((bf16[3,256,4,192]{1,3,0,2:T(8,128)(2,1)}), bf16[3,256,4,192]{1,3,0,2:T(8,128)(2,1)}, u32[]{:S(2)}, u32[]{:S(2)}) async-start(bf16[3,256,4,192]{1,3,0,2:T(8,128)(2,1)} %copy.79), calls=%async_computation.2 | async-start | bytes 2359296 | tf_op jit(solution)/shard_map/all_to_all | solution.py:144
  318.3 290.7 %reduce-scatter.7.cloned.1.call-start = ((), (), s32[]{:S(2)}) async-start(), calls=%async_computation.13 | async-start | bytes 2654208 | tf_op jit(solution)/shard_map/reduce_scatter | solution.py:184
  325.2 319.5 %reduce-scatter.5.cloned.1.call-start = ((), (), s32[]{:S(2)}) async-start(), calls=%async_computation.12 | async-start | bytes 7962624 | tf_op jit(solution)/shard_map/reduce_scatter | solution.py:183
  341.2 8.6 copy-start.8
  341.2 8.7 copy-start.21
  349.9 15.7 %copy-start.22 = (f32[3,3,512]{2,1,0:T(4,128)S(1)}, f32[3,3,512]{2,1,0:T(4,128)}, u32[]{:S(2)}) copy-start(f32[3,3,512]{2,1,0:T(4,128)} %log_add_fusion.1) | copy-start | bytes 55300
  394.1 3.1 copy-start.14
  502.3 8.0 copy-start.1
  502.3 8.0 copy-start.10
  502.3 8.0 copy-start.24
  502.3 8.0 copy-start.27
  518.0 1.3 copy-start.7
  518.0 293.3 %reduce-scatter.11.cloned.1.call-start = ((), (), s32[]{:S(2)}) async-start(), calls=%async_computation.15 | async-start | bytes 10616832 | tf_op jit(solution)/shard_map/reduce_scatter | solution.py:186
  532.7 445.1 %reduce-scatter.9.cloned.1.call-start = ((), (), s32[]{:S(2)}) async-start(), calls=%async_computation.14 | async-start | bytes 10616832 | tf_op jit(solution)/shard_map/reduce_scatter | solution.py:185
  543.6 1.2 copy-start.38
  543.6 484.0 %all-reduce.4.cloned.1.call-start = ((), (), s32[]{:S(2)}) async-start(), calls=%async_computation.16 | async-start | bytes 3538944 | tf_op jit(solution)/shard_map/psum | solution.py:189
  560.5 8.2 copy-start.33
  560.5 47.7 %copy-start.31 = (f32[768]{0:T(1024)S(1)}, f32[768]{0:T(1024)}, u32[]{:S(2)}) copy-start(f32[768]{0:T(1024)} %copy-done.30) | copy-start | bytes 9220
  980.0 2.7 copy-start.3
  980.1 2.7 copy-start.29
  1027.6 5.9 copy-start.20
Sparse Core Ops, SparseCore 0:
  10.8 67.8 all-gather.4
  81.5 39.5 all-gather.6
  123.2 78.6 all-gather.8
  204.0 77.9 all-gather.10
  325.3 67.4 reduce-scatter.6
  518.1 126.5 reduce-scatter.4
  648.7 162.5 reduce-scatter.10
  815.3 162.5 reduce-scatter.8
  981.8 45.7 all-reduce.3
where the time goes:
time: 1050 us; the launch traced here: 1040 us
  waiting for transfers between devices  518 us (49%)
  matrix products  194 us (18%)
  blocking collectives  131 us (12%)
  other arithmetic  96.7 us (9%)
  local copies, waits for them, and re-layouts  78 us (7%)
  between operations  14.8 us (1%)
    reduce_scatter x1, waiting for transfers between devices, local(): lax.psum_scatter(proj_grad, 'fsdp', scatter_dimension=0, tiled=True)  165 us
    reduce_scatter x1, waiting for transfers between devices, local(): lax.psum_scatter(fc_grad, 'fsdp', scatter_dimension=0, tiled=True)  164 us
    all_to_all x1, blocking collectives, local(): lax.all_to_all(d_packed, 'seq', split_axis=1, concat_axis=2, tiled=True)  63.3 us
    all_gather x1, waiting for transfers between devices, local(): lax.all_gather(qkv_weight.astype(jnp.bfloat16), 'fsdp', axis=0, tiled=True)  63.1 us
    psum x1, waiting for transfers between devices, local(): lax.psum(qkv_share.astype(jnp.bfloat16), 'seq').astype(jnp.float32)  42.9 us
    psum x1, blocking collectives, local(): lax.psum((gain_one_grad, qv_bias_grad, out_bias_grad, gain_two_grad, fc_b...  39.5 us
    all_to_all x1, waiting for transfers between devices, local(): lax.all_to_all(packed, 'seq', split_axis=2, concat_axis=1, tiled=True)  34.3 us
    reduce_scatter x1, waiting for transfers between devices, local(): lax.psum_scatter(qkv_grad, 'fsdp', scatter_dimension=0, tiled=True)  34.1 us
  transfers between devices with their start and end apart: 11, of which 8 were waited for; matrix products, arithmetic and copies ran while one was open for 31% of the time, Pallas kernels for 0%

commit v1 on v0

--- a/solution.py
+++ b/solution.py
@@ -103,7 +103,9 @@
         )
     attended = jnp.concatenate(outputs_list, axis=1).astype(jnp.bfloat16)
     attended = attended.reshape(seq_count, full_len, my_heads * head_dim)
-    by_tokens = lax.all_to_all(attended, "seq", split_axis=1, concat_axis=2, tiled=True)
+    pieces = jnp.split(attended, lax.axis_size("seq"), axis=1)
+    received = lax.all_to_all(jnp.stack(pieces), "seq", 0, 0)
+    by_tokens = jnp.concatenate(received, axis=2)
     attn_flat = by_tokens.reshape(token_count, width)
     middle = (
         resid_flat + jnp.dot(attn_flat, out_matrix, preferred_element_type=jnp.float32) + out_bias

time: 1050 us -> 1050 us (level)
  waiting for transfers between devices: 518 us -> 535 us
    all_gather x1, waiting for transfers between devices: 5.49 us -> 22.7 us  [local(): lax.all_gather(proj_weight.astype(jnp.bfloat16), 'fsdp', axis=0, tiled=True)]
  transfers between devices with their start and end apart: 11 -> 11, of which waited for: 8 -> 8; matrix products, arithmetic and copies ran while one was open for 31% -> 30% of each run, Pallas kernels for 0% -> 0%
where the time goes in v1:
time: 1050 us; the launch traced here: 1040 us
  waiting for transfers between devices  535 us (51%)
  matrix products  192 us (18%)
  blocking collectives  122 us (12%)
  other arithmetic  94.1 us (9%)
  local copies, waits for them, and re-layouts  74.9 us (7%)
  between operations  14.6 us (1%)
    reduce_scatter x1, waiting for transfers between devices, local(): lax.psum_scatter(fc_grad, 'fsdp', scatter_dimension=0, tiled=True)  164 us
    reduce_scatter x1, waiting for transfers between devices, local(): lax.psum_scatter(proj_grad, 'fsdp', scatter_dimension=0, tiled=True)  164 us
    all_to_all x1, blocking collectives, local(): lax.all_to_all(d_packed, 'seq', split_axis=1, concat_axis=2, tiled=True)  63.3 us
    all_gather x1, waiting for transfers between devices, local(): lax.all_gather(qkv_weight.astype(jnp.bfloat16), 'fsdp', axis=0, tiled=True)  63.1 us
    psum x1, waiting for transfers between devices, local(): lax.psum(qkv_share.astype(jnp.bfloat16), 'seq').astype(jnp.float32)  42.9 us
    psum x1, blocking collectives, local(): lax.psum((gain_one_grad, qv_bias_grad, out_bias_grad, gain_two_grad, fc_b...  39.7 us
    all_to_all x1, waiting for transfers between devices, local(): lax.all_to_all(packed, 'seq', split_axis=2, concat_axis=1, tiled=True)  34.3 us
    reduce_scatter x1, waiting for transfers between devices, local(): lax.psum_scatter(qkv_grad, 'fsdp', scatter_dimension=0, tiled=True)  34 us
  transfers between devices with their start and end apart: 11, of which 8 were waited for; matrix products, arithmetic and copies ran while one was open for 30% of the time, Pallas kernels for 0%

profile of v1, /device:TPU:0, one launch (start us, length us, event | category | flops | bytes accessed | tf_op | source)
XLA Modules:
  0.0 1041.8 jit_solution(2397170289816866010)
XLA Ops:
  7.2 2.1 convert_element_type.113
  15.6 63.1 %all-gather.5.cloned.1.call-done = bf16[768,2304]{1,0:T(8,128)(2,1)} async-done(((bf16[96,2304]{1,0:T(8,128)(2,1)}), bf16[768,2304]{1,0:T(8,128)(2,1)}) %all-gather.5.cloned.1.call-update) | async-done | bytes 3538960 | tf_op jit(solution)/shard_map/all_gather | solution.py:64
  78.7 6.6 add_convert_fusion
  85.3 9.1 reshape.214
  94.4 7.8 copy.70
  102.3 3.7 all-to-all-start
  106.1 2.1 convert_element_type.122
  109.1 3.8 compare_and_fusion.1
  112.9 34.3 %all-to-all-done = bf16[3,256,4,576]{1,3,0,2:T(8,128)(2,1)S(1)} async-done(((bf16[3,256,4,576]{1,3,0,2:T(8,128)(2,1)}), bf16[3,256,4,576]{1,3,0,2:T(8,128)(2,1)S(1)}, u32[]{:S(2)}, u32[]{:S(2)}) %all-to-all-start) | async-done | bytes 3538976 | tf_op jit(solution)/shard_map/all_to_all | solution.py:79
  147.1 4.5 copy.71
  151.7 6.1 reshape.215
  157.9 1.8 copy-done.19
  159.7 9.2 fusion.57
  168.9 10.1 fusion.1
  179.0 8.5 fusion.28
  188.4 9.5 fusion.58
  197.9 10.0 fusion
  207.9 9.0 fusion.29
  217.1 19.4 %all_to_all.50 = bf16[4,3,256,192]{2,3,1,0:T(8,128)(2,1)} all-to-all(bf16[4,3,256,192]{2,3,1,0:T(8,128)(2,1)S(1)} %pad_maximum_fusion.3), channel_id=1, replica_groups=mesh['fsdp'=8,'seq'=4] {'seq'}, dimensions={0} | all-to-all | bytes 2359296 | tf_op jit(solution)/shard_map/all_to_all | solution.py:107
  236.5 3.7 copy.75
  240.2 4.0 reshape_reshape.3
  244.2 3.2 fusion.59
  249.2 10.7 %fusion.51 = f32[768,3072]{1,0:T(8,128)} fusion(bf16[768,3072]{1,0:T(8,128)(2,1)} %all-gather.9.cloned.1.call-done, f32[768]{0:T(1024)S(1)} %copy-done.29, f32[768]{0:T(1024)S(1)} %fusion.48, f32[768,1]{1,0:T(8,128)} %copy-done.11, f32[768,767]{1,0:T(8,128)} %copy-done.4), kind=kOutput, calls=%fused_computation.121 | convolution fusion | flops 3626237952 | bytes 16521216 | tf_op jit(solution)/shard_map/dot_general | solution.py:114
  259.9 22.7 %all-gather.11.cloned.1.call-done = bf16[3072,767]{1,0:T(8,128)(2,1)} async-done(((bf16[384,767]{1,0:T(8,128)(2,1)}), bf16[3072,767]{1,0:T(8,128)(2,1)}) %all-gather.11.cloned.1.call-update) | async-done | bytes 4712464 | tf_op jit(solution)/shard_map/all_gather | solution.py:67
  282.6 13.7 %convert_reduce_fusion = (f32[3072]{0:T(1024)}, bf16[768,3072]{1,0:T(8,128)(2,1)S(1)}) fusion(f32[768,3072]{1,0:T(8,128)} %fusion.51, f32[3072]{0:T(1024)} %param.23, bf16[768,767]{1,0:T(8,128)(2,1)} %bitcast.121, bf16[3072,767]{1,0:T(8,128)(2,1)} %all-gather.11.cloned.1.call-done), kind=kOutput, calls=%fused_computation.27 | convolution fusion | flops 3673420800 | bytes 20070912 | tf_op jit(solution)/shard_map/tc,fc->tf/dot_general | solution.py:128
  296.3 4.8 multiply_reduce_fusion.2
  304.5 2.2 convolution_convert_fusion
  306.6 4.4 reshape.219
  311.0 3.5 copy.77
  314.6 4.3 all-to-all-start.2
  321.7 4.1 fusion.60
  325.9 8.9 all-to-all-done.2
  334.8 3.2 copy.78
  338.0 3.6 reshape.220
  341.6 8.6 fusion.11
  350.3 15.7 %multiply_reduce_fusion = (f32[3,3,512]{2,1,0:T(4,128)S(1)}, f32[3,3,512,1024]{3,2,1,0:T(8,128)}) fusion(f32[3,3,512,1024]{3,2,1,0:T(8,128)} %get-tuple-element.45, f32[3,3,512]{2,1,0:T(4,128)S(1)} %copy-done.25, bf16[3,1024,3,3,64]{1,4,3,2,0:T(8,128)(2,1)S(1)} %reshape.215, bf16[3,1024,3,64]{1,3,2,0:T(8,128)(2,1)S(1)} %copy-done.8), kind=kOutput, calls=%fused_computation.1 | convolution fusion | flops 618130944 | bytes 39561216 | tf_op jit(solution)/shard_map/bqhe,bkhe->bhqk/dot_general | solution.py:157
  366.0 15.5 %multiply_reduce_fusion.1 = (f32[3,3,512]{2,1,0:T(4,128)S(1)}, f32[3,3,512,1024]{3,2,1,0:T(8,128)}) fusion(f32[3,3,512,1024]{3,2,1,0:T(8,128)} %get-tuple-element.47, f32[3,3,512]{2,1,0:T(4,128)S(1)} %copy-done.26, bf16[3,1024,3,3,64]{1,4,3,2,0:T(8,128)(2,1)S(1)} %reshape.215, bf16[3,1024,3,64]{1,3,2,0:T(8,128)(2,1)S(1)} %copy-done.8), kind=kOutput, calls=%fused_computation.4 | convolution fusion | flops 618130944 | bytes 39561216 | tf_op jit(solution)/shard_map/bqhe,bkhe->bhqk/dot_general | solution.py:157
  381.4 13.1 %multiply_convert_fusion.1 = bf16[3,3,512,1024]{3,2,1,0:T(8,128)(2,1)S(1)} fusion(f32[3,3,512,1024]{3,2,1,0:T(8,128)} %get-tuple-element.52, f32[3,3,512,1024]{3,2,1,0:T(8,128)} %get-tuple-element.47, f32[3,3,512]{2,1,0:T(4,128)S(1)} %get-tuple-element.51, f32[3,3,512]{2,1,0:T(4,128)S(1)} %copy-done.26), kind=kLoop, calls=%fused_computation.3 | loop fusion | flops 18874368 | bytes 47222784 | tf_op jit(solution)/shard_map/convert_element_type | solution.py:161
  394.5 3.0 fusion.33
  399.4 8.3 fusion.24
  407.7 13.3 %multiply_convert_fusion = bf16[3,3,512,1024]{3,2,1,0:T(8,128)(2,1)S(1)} fusion(f32[3,3,512,1024]{3,2,1,0:T(8,128)} %get-tuple-element.54, f32[3,3,512,1024]{3,2,1,0:T(8,128)} %get-tuple-element.45, f32[3,3,512]{2,1,0:T(4,128)S(1)} %get-tuple-element.53, f32[3,3,512]{2,1,0:T(4,128)S(1)} %copy-done.25), kind=kLoop, calls=%fused_computation | loop fusion | flops 18874368 | bytes 47222784 | tf_op jit(solution)/shard_map/convert_element_type | solution.py:161
  421.0 3.0 fusion.32
  424.2 1.8 fusion.23
  426.9 6.3 copy.80
  433.1 63.3 %all_to_all.51 = bf16[3,1024,576]{2,0,1:T(4,128)(2,1)S(1)} all-to-all(bf16[3,1024,576]{2,0,1:T(4,128)(2,1)} %copy.80), channel_id=1, replica_groups=mesh['fsdp'=8,'seq'=4] {'seq'}, dimensions={1} | all-to-all | bytes 7077888 | tf_op jit(solution)/shard_map/all_to_all | solution.py:175
  496.4 6.7 convert_reduce_fusion.1
  503.1 8.0 reshape.221
  511.0 7.6 fusion.49
  519.9 13.4 %fusion.52 = f32[3072,767]{1,0:T(8,128)} fusion(bf16[768,767]{1,0:T(8,128)(2,1)S(1)} %bitcast.122, f32[768,3072]{1,0:T(8,128)} %fusion.51, f32[3072]{0:T(1024)} %param.23), kind=kOutput, calls=%fused_computation.122 | convolution fusion | flops 3642753024 | bytes 20052480 | tf_op jit(solution)/shard_map/tf,tc->fc/dot_general | solution.py:126
  533.5 10.8 %fusion.50 = f32[768,3072]{1,0:T(8,128)} fusion(bf16[768,3072]{1,0:T(8,128)(2,1)} %copy-done.16, f32[768]{0:T(1024)S(1)} %copy-done.29, f32[768]{0:T(1024)S(1)} %fusion.48, f32[768,1]{1,0:T(8,128)} %copy-done.11, f32[768,767]{1,0:T(8,128)} %copy-done.4), kind=kOutput, calls=%fused_computation.120 | convolution fusion | flops 3626237952 | bytes 16521216 | tf_op jit(solution)/shard_map/td,tf->df/dot_general | solution.py:131
  545.4 12.8 %add_convert_fusion.2 = bf16[768,767]{1,0:T(8,128)(2,1)} fusion(f32[768,767]{1,0:T(8,128)} %copy-done.4, bf16[3072,767]{1,0:T(8,128)(2,1)} %all-gather.11.cloned.1.call-done, f32[767]{0:T(1024)S(1)} %copy-done.42, f32[768,3072]{1,0:T(8,128)} %fusion.51, f32[3072]{0:T(1024)} %param.23), kind=kOutput, calls=%fused_computation.55 | convolution fusion | flops 3644520192 | bytes 17699324 | tf_op jit(solution)/shard_map/dot_general | solution.py:116
  561.2 8.2 multiply_reduce_fusion.3
  569.4 39.7 %all-reduce = (f32[768]{0:T(1024)}, f32[12,128]{1,0:T(8,128)}, f32[767]{0:T(1024)}, f32[768]{0:T(1024)}, f32[3072]{0:T(1024)}, /*index=5*/f32[767]{0:T(1024)}) all-reduce(f32[768]{0:T(1024)} %get-tuple-element.14, f32[12,128]{1,0:T(8,128)} %pad_maximum_fusion.5, ...), channel_id=1, replica_groups=mesh['fsdp'=8,'seq'=4] {'fsdp','seq'}, use_global_device_ids=true, to_apply=%region_15.16 | all-reduce | flops 7678 | bytes 61424 | tf_op jit(solution)/shard_map/psum | solution.py:196
  611.4 34.0 %reduce-scatter.5.cloned.1.call-done = f32[96,2304]{1,0:T(8,128)} async-done(((f32[768,2304]{1,0:T(8,128)}), f32[96,2304]{1,0:T(8,128)}) %reduce-scatter.5.cloned.1.call-update) | async-done | bytes 884752 | tf_op jit(solution)/shard_map/reduce_scatter | solution.py:185
  645.4 2.0 convert_element_type.133
  647.4 164.4 %reduce-scatter.11.cloned.1.call-done = f32[384,767]{1,0:T(8,128)} async-done(((f32[3072,767]{1,0:T(8,128)}), f32[384,767]{1,0:T(8,128)}) %reduce-scatter.11.cloned.1.call-update) | async-done | bytes 1178128 | tf_op jit(solution)/shard_map/reduce_scatter | solution.py:188
  811.8 2.1 convert_element_type.142
  813.9 164.5 %reduce-scatter.9.cloned.1.call-done = f32[96,3072]{1,0:T(8,128)} async-done(((f32[768,3072]{1,0:T(8,128)}), f32[96,3072]{1,0:T(8,128)}) %reduce-scatter.9.cloned.1.call-update) | async-done | bytes 1179664 | tf_op jit(solution)/shard_map/reduce_scatter | solution.py:187
  978.4 2.2 convert_element_type.139
  980.6 2.4 add_add_fusion
  983.3 1.9 fusion.19
  985.2 42.9 %all-reduce.4.cloned.1.call-done = (bf16[96,2304]{1,0:T(8,128)(2,1)}, bf16[96,767]{1,0:T(8,128)(2,1)}, bf16[96,3072]{1,0:T(8,128)(2,1)}, bf16[384,767]{1,0:T(8,128)(2,1)}) async-done(((bf16[96,2304]{1,0:T(8,128)(2,1)}, bf16[96,767]{1,0:T(8,128)(2,1)}, bf16[96,3072]{1,0:T(8,128)(2,1)}, bf16[384,767]{1,0:T(8,128)(2,1)}), (bf16[96,2304]{1,0:T(8,128)(2,1)}, bf16[96,767]{1,0:T(8,128)(2,1)}, ...) | async-done | bytes 1768528 | tf_op jit(solution)/shard_map/psum | solution.py:191
  1029.8 2.0 convert_element_type.134
  1031.8 2.2 convert_element_type.140
  (156 shorter events, 29.8 us)
Async XLA Ops:
  7.2 4.0 copy-start.22
  7.2 4.9 copy-start.17
  7.2 71.5 %all-gather.5.cloned.1.call-start = ((), (), s32[]{:S(2)}) async-start(), calls=%async_computation.8 | async-start | bytes 3981312 | tf_op jit(solution)/shard_map/all_gather | solution.py:64
  9.4 3.0 copy-start.36
  9.4 234.8 %all-gather.7.cloned.1.call-start = ((), (), s32[]{:S(2)}) async-start(), calls=%async_computation.9 | async-start | bytes 1327104 | tf_op jit(solution)/shard_map/all_gather | solution.py:65
  11.1 238.1 %all-gather.9.cloned.1.call-start = ((), (), s32[]{:S(2)}) async-start(), calls=%async_computation.10 | async-start | bytes 5308416 | tf_op jit(solution)/shard_map/all_gather | solution.py:66
  12.9 65.9 %copy-start.9 = (f32[1,768]{0,1:T(8,128)}, f32[1,768]{0,1:T(8,128)S(1)}, u32[]{:S(2)}) copy-start(f32[1,768]{0,1:T(8,128)S(1)} %copy.89) | copy-start | bytes 9220
  12.9 65.8 %copy-start.30 = (f32[768]{0:T(1024)S(1)}, f32[768]{0:T(1024)}, u32[]{:S(2)}) copy-start(f32[768]{0:T(1024)} %param.16) | copy-start | bytes 9220
  14.5 70.8 %copy-start = (f32[768,767]{1,0:T(8,128)}, f32[768,767]{1,0:T(8,128)S(1)}, u32[]{:S(2)}) copy-start(f32[768,767]{1,0:T(8,128)S(1)} %convert.50) | copy-start | bytes 7068676
  14.8 0.8 copy-start.34
  15.6 69.7 %copy-start.27 = (f32[768]{0:T(1024)}, f32[768]{0:T(1024)S(1)}, u32[]{:S(2)}) copy-start(f32[768]{0:T(1024)S(1)} %fusion.47) | copy-start | bytes 9220
  102.3 44.9 %all-to-all-start = ((bf16[3,256,4,576]{1,3,0,2:T(8,128)(2,1)}), bf16[3,256,4,576]{1,3,0,2:T(8,128)(2,1)S(1)}, u32[]{:S(2)}, u32[]{:S(2)}) async-start(bf16[3,256,4,576]{1,3,0,2:T(8,128)(2,1)} %copy.70), calls=%async_computation | async-start | bytes 7077888 | tf_op jit(solution)/shard_map/all_to_all | solution.py:79
  106.0 2.2 copy-start.38
  106.0 176.6 %all-gather.11.cloned.1.call-start = ((), (), s32[]{:S(2)}) async-start(), calls=%async_computation.11 | async-start | bytes 5308416 | tf_op jit(solution)/shard_map/all_gather | solution.py:67
  157.7 2.0 copy-start.19
  157.9 11.1 %copy-start.13 = (bf16[3,1024,3,64]{1,3,2,0:T(8,128)(2,1)}, bf16[3,1024,3,64]{1,3,2,0:T(8,128)(2,1)S(1)}, u32[]{:S(2)}) copy-start(bf16[3,1024,3,64]{1,3,2,0:T(8,128)(2,1)S(1)} %slice_bitcast_fusion.1) | copy-start | bytes 3538948
  179.0 9.4 copy-start.14
  179.0 9.4 copy-start.18
  207.9 9.0 copy-start.20
  207.9 9.0 copy-start.21
  236.5 7.7 copy-start.41
  247.4 1.4 copy-start.4
  247.4 1.8 copy-start.29
  247.6 1.5 copy-start.11
  282.6 13.7 %copy-start.5 = (f32[768,767]{1,0:T(8,128)S(1)}, f32[768,767]{1,0:T(8,128)}, u32[]{:S(2)}) copy-start(f32[768,767]{1,0:T(8,128)} %copy-done.4) | copy-start | bytes 7068676
  282.6 13.7 %copy-start.12 = (f32[768,1]{1,0:T(8,128)S(1)}, f32[768,1]{1,0:T(8,128)}, u32[]{:S(2)}) copy-start(f32[768,1]{1,0:T(8,128)} %copy-done.11) | copy-start | bytes 9220
  282.6 13.7 %copy-start.39 = (bf16[768,3072]{1,0:T(8,128)(2,1)S(1)}, bf16[768,3072]{1,0:T(8,128)(2,1)}, u32[]{:S(2)}) copy-start(bf16[768,3072]{1,0:T(8,128)(2,1)} %all-gather.9.cloned.1.call-done) | copy-start | bytes 14155780
  296.3 4.8 copy-start.16
  301.1 1.3 copy-start.6
  301.7 1.7 copy-start.2
  302.4 1.1 copy-start.32
  302.4 2.1 copy-start.40
  303.4 1.0 copy-start.23
  314.6 20.2 %all-to-all-start.2 = ((bf16[3,256,4,192]{1,3,0,2:T(8,128)(2,1)}), bf16[3,256,4,192]{1,3,0,2:T(8,128)(2,1)}, u32[]{:S(2)}, u32[]{:S(2)}) async-start(bf16[3,256,4,192]{1,3,0,2:T(8,128)(2,1)} %copy.77), calls=%async_computation.2 | async-start | bytes 2359296 | tf_op jit(solution)/shard_map/all_to_all | solution.py:146
  318.9 290.9 %reduce-scatter.7.cloned.1.call-start = ((), (), s32[]{:S(2)}) async-start(), calls=%async_computation.13 | async-start | bytes 2654208 | tf_op jit(solution)/shard_map/reduce_scatter | solution.py:186
  325.8 319.6 %reduce-scatter.5.cloned.1.call-start = ((), (), s32[]{:S(2)}) async-start(), calls=%async_computation.12 | async-start | bytes 7962624 | tf_op jit(solution)/shard_map/reduce_scatter | solution.py:185
  341.6 8.7 copy-start.8
  341.6 8.7 copy-start.25
  350.2 15.7 %copy-start.26 = (f32[3,3,512]{2,1,0:T(4,128)S(1)}, f32[3,3,512]{2,1,0:T(4,128)}, u32[]{:S(2)}) copy-start(f32[3,3,512]{2,1,0:T(4,128)} %log_add_fusion.1) | copy-start | bytes 55300
  394.5 3.1 copy-start.15
  503.1 8.0 copy-start.1
  503.1 8.0 copy-start.10
  503.1 8.0 copy-start.28
  503.1 8.0 copy-start.31
  518.7 1.3 copy-start.7
  518.7 293.1 %reduce-scatter.11.cloned.1.call-start = ((), (), s32[]{:S(2)}) async-start(), calls=%async_computation.15 | async-start | bytes 10616832 | tf_op jit(solution)/shard_map/reduce_scatter | solution.py:188
  533.4 445.0 %reduce-scatter.9.cloned.1.call-start = ((), (), s32[]{:S(2)}) async-start(), calls=%async_computation.14 | async-start | bytes 10616832 | tf_op jit(solution)/shard_map/reduce_scatter | solution.py:187
  544.3 1.1 copy-start.42
  544.3 483.8 %all-reduce.4.cloned.1.call-start = ((), (), s32[]{:S(2)}) async-start(), calls=%async_computation.16 | async-start | bytes 3538944 | tf_op jit(solution)/shard_map/psum | solution.py:191
  561.1 8.2 copy-start.37
  561.1 47.9 %copy-start.35 = (f32[768]{0:T(1024)S(1)}, f32[768]{0:T(1024)}, u32[]{:S(2)}) copy-start(f32[768]{0:T(1024)} %copy-done.34) | copy-start | bytes 9220
  980.6 2.7 copy-start.3
  980.6 2.7 copy-start.33
  1028.1 5.9 copy-start.24
Sparse Core Ops, SparseCore 0:
  10.8 67.8 all-gather.4
  80.9 39.5 all-gather.6
  123.2 78.6 all-gather.8
  204.5 78.0 all-gather.10
  326.0 67.6 reduce-scatter.6
  518.8 126.5 reduce-scatter.4
  649.4 162.3 reduce-scatter.10
  815.8 162.5 reduce-scatter.8
  982.4 45.6 all-reduce.3
